TPU v7x, 256 devices: a whole 4x4x8 slice. The times are simulated.
256 devices in a mesh: dp: 8 (over z_lo, y), seq: 32 (over x, z_hi, core).
Axes of the slice: x: 4, y: 4, z: 8 (z_hi: 4, z_lo: 2; z = z_hi * 2 + z_lo), core: 2. Of those that a mesh axis runs over, the one named last changes fastest.
Arguments:
- tokens: bfloat16 [8, 8192, 4096], P('dp', 'seq'), may hold values from -6 to 6
- queries: bfloat16 [8, 8192, 128], P('dp', 'seq'), may hold values from -6 to 6
- key_vectors: bfloat16 [8, 8192, 128], P('dp', 'seq'), may hold values from -6 to 6
- doc_position: int32 [8, 8192], P('dp', 'seq'), may hold values from 0 to 8191, as said below
- value_scores: float32 [8, 8192, 4], P('dp', 'seq'), may hold values from 0.1 to 1
- value_experts: int32 [8, 8192, 2], P('dp', 'seq'), may hold values from 0 to 3, all different within a row
- output_scores: float32 [8, 8192, 4], P('dp', 'seq'), may hold values from 0.1 to 1
- output_experts: int32 [8, 8192, 2], P('dp', 'seq'), may hold values from 0 to 3, all different within a row
- value_panels: bfloat16 [4096, 512], P('seq'), may hold values from -0.09375 to 0.09375
- output_panels: bfloat16 [4096, 512], P('seq'), may hold values from -3 to 3
- cotangent: bfloat16 [8, 8192, 4096], P('dp', 'seq'), may hold values from -0.625 to 0.625
Outputs:
- layer_output: bfloat16 [8, 8192, 4096], P('dp', 'seq')
- grad_tokens: bfloat16 [8, 8192, 4096], P('dp', 'seq')
- grad_queries: bfloat16 [8, 8192, 128], P('dp', 'seq')
- grad_keys: bfloat16 [8, 8192, 128], P('dp', 'seq')
- grad_value: float32 [4096, 512], P('seq')
- grad_output: float32 [4096, 512], P('seq')
Inputs may be any that keep to these rules, and one draw needn't show every extreme that they name: doc_position[b, i] is i minus the first position of the document that holds position i; position 0 starts a document in every sequence; sequence 0 is one document; every other sequence holds one to four documents.
All inputs are finite; a program needn't handle non-finite values.
Results may differ from a plain program's by a relative error of at most 0.035.
Values may be sent and summed in bfloat16 or wider, within the bound.
No kernel may reach another device: no remote copies, remote signals or barrier semaphores. Data moves between devices by JAX's collectives and lax.ppermute only.
A program may use at most 128 MiB of HBM per device.

v0:
```python
import jax
import jax.numpy as jnp
from jax import lax
from jax.sharding import PartitionSpec as P


def expert_gates(scores, chosen, experts):
    chosen_hit = chosen[:, :, None] == lax.iota(jnp.int32, experts)[None, None, :]
    return jnp.where(jnp.any(chosen_hit, axis=1), scores, jnp.float32(0.0))


def contract_last(left, right):
    return lax.dot_general(
        left, right, (((1,), (1,)), ((), ())), preferred_element_type=jnp.float32
    )


def contract_first(left, right):
    return lax.dot_general(
        left, right, (((0,), (0,)), ((), ())), preferred_element_type=jnp.float32
    )


def body(
    tokens,
    queries,
    key_vectors,
    doc_position,
    value_scores,
    value_experts,
    output_scores,
    output_experts,
    value_panels,
    output_panels,
    cotangent,
):
    tok_block = tokens[0]
    query_block = queries[0]
    own_keys = key_vectors[0]
    positions = doc_position[0]
    grad_rows = cotangent[0]
    tok_rows = tok_block.shape[0]
    head_size = query_block.shape[1]
    experts = value_scores.shape[2]
    panel_width = value_panels.shape[1]
    value_gate = expert_gates(value_scores[0], value_experts[0], experts)
    output_gate = expert_gates(output_scores[0], output_experts[0], experts)
    value_full, output_full = (
        lax.all_gather(value_panels, "seq", axis=0, tiled=True),
        lax.all_gather(output_panels, "seq", axis=0, tiled=True),
    )
    projection = jnp.dot(tok_block, value_full, preferred_element_type=jnp.float32)
    value_vec = jnp.sum(
        projection.reshape(tok_rows, experts, head_size) * value_gate[:, :, None], axis=1
    ).astype(jnp.bfloat16)
    keys_all, values_all = (
        lax.all_gather(own_keys, "seq", axis=0, tiled=True),
        lax.all_gather(value_vec, "seq", axis=0, tiled=True),
    )
    length = keys_all.shape[0]
    score_scale = head_size ** (-0.5)
    query_index = lax.axis_index("seq") * tok_rows + lax.iota(jnp.int32, tok_rows)
    key_index = lax.iota(jnp.int32, length)
    visible = (key_index[None, :] <= query_index[:, None]) & (
        query_index[:, None] - key_index[None, :] <= positions[:, None]
    )
    masked = jnp.where(visible, contract_last(query_block, keys_all) * score_scale, -jnp.inf)
    row_max = jnp.max(masked, axis=1)
    log_total = row_max + jnp.log(jnp.sum(jnp.exp(masked - row_max[:, None]), axis=1))
    attn_prob = jnp.exp(masked - log_total[:, None])
    prob_low = attn_prob.astype(jnp.bfloat16)
    attended = jnp.dot(prob_low, values_all, preferred_element_type=jnp.float32).astype(
        jnp.bfloat16
    )
    expanded = (
        (output_gate[:, :, None] * attended.astype(jnp.float32)[:, None, :])
        .reshape(tok_rows, panel_width)
        .astype(jnp.bfloat16)
    )
    layer_output = contract_last(expanded, output_full).astype(jnp.bfloat16)
    pulled = jnp.dot(grad_rows, output_full, preferred_element_type=jnp.float32)
    dattended = jnp.sum(
        pulled.reshape(tok_rows, experts, head_size) * output_gate[:, :, None], axis=1
    ).astype(jnp.bfloat16)
    row_delta = jnp.sum(dattended.astype(jnp.float32) * attended.astype(jnp.float32), axis=1)
    dweights = contract_last(dattended, values_all)
    dscores = (attn_prob * (dweights - row_delta[:, None])).astype(jnp.bfloat16)
    grad_queries = (
        jnp.dot(dscores, keys_all, preferred_element_type=jnp.float32) * score_scale
    ).astype(jnp.bfloat16)
    key_term = contract_first(dscores, query_block) * score_scale
    value_term = contract_first(prob_low, dattended)
    dkey_sum, dvalue_sum = (
        lax.psum_scatter(
            key_term.astype(jnp.bfloat16), "seq", scatter_dimension=0, tiled=True
        ).astype(jnp.float32),
        lax.psum_scatter(
            value_term.astype(jnp.bfloat16), "seq", scatter_dimension=0, tiled=True
        ).astype(jnp.float32),
    )
    grad_keys = dkey_sum.astype(jnp.bfloat16)
    dvalue = dvalue_sum.astype(jnp.bfloat16)
    value_grad = (
        (value_gate[:, :, None] * dvalue.astype(jnp.float32)[:, None, :])
        .reshape(tok_rows, panel_width)
        .astype(jnp.bfloat16)
    )
    grad_tokens = contract_last(value_grad, value_full).astype(jnp.bfloat16)
    term_value = contract_first(tok_block, value_grad)
    term_output = contract_first(grad_rows, expanded)
    owned = lax.psum_scatter(
        jnp.concatenate([term_value, term_output], axis=1).astype(jnp.bfloat16),
        "seq",
        scatter_dimension=0,
        tiled=True,
    )
    summed = lax.psum(owned, "dp").astype(jnp.float32)
    return (
        layer_output[None],
        grad_tokens[None],
        grad_queries[None],
        grad_keys[None],
        summed[:, :panel_width],
        summed[:, panel_width:],
    )


def solution(mesh):
    in_specs = (
        P("dp", "seq", None),
        P("dp", "seq", None),
        P("dp", "seq", None),
        P("dp", "seq"),
        P("dp", "seq", None),
        P("dp", "seq", None),
        P("dp", "seq", None),
        P("dp", "seq", None),
        P("seq", None),
        P("seq", None),
        P("dp", "seq", None),
    )
    out_specs = (
        P("dp", "seq", None),
        P("dp", "seq", None),
        P("dp", "seq", None),
        P("dp", "seq", None),
        P("seq", None),
        P("seq", None),
    )
    return jax.shard_map(body, mesh=mesh, in_specs=in_specs, out_specs=out_specs, check_vma=False)
```

profile of v0, /device:TPU:8, one launch (start us, length us, event | category | flops | bytes accessed | tf_op | source)
XLA Modules:
  0.0 667.2 jit_solution(10940611194924719588)
XLA Ops:
  7.2 0.0 copy-start
  7.2 0.0 all-gather.12.cloned.1.call-start
  7.2 0.7 all-gather.12.cloned.1.call-update
  7.9 0.0 all-gather.10.cloned.1.call-start
  8.0 0.7 all-gather.10.cloned.1.call-update
  8.7 0.0 all-gather.6.cloned.1.call-start
  8.7 0.7 all-gather.6.cloned.1.call-update
  9.4 0.0 reduce-scatter.6.cloned.1.call-start
  9.5 0.7 fusion.43
  10.2 0.7 bitcast_select_fusion.1
  10.9 57.3 %all-gather.12.cloned.1.call-done = bf16[1,8192,128]{2,1,0:T(8,128)(2,1)} async-done(((bf16[1,256,128]{2,1,0:T(8,128)(2,1)}), bf16[1,8192,128]{2,1,0:T(8,128)(2,1)}) %all-gather.12.cloned.1.call-update) | async-done | bytes 2097168 | tf_op jit(solution)/shard_map/all_gather | solution.py:57
  68.2 4.6 fusion.50
  72.8 1.3 exponential_reduce_fusion
  74.1 1.9 copy-done.2
  76.0 52.1 %all-gather.10.cloned.1.call-done = bf16[4096,512]{1,0:T(8,128)(2,1)} async-done(((bf16[128,512]{1,0:T(8,128)(2,1)}), bf16[4096,512]{1,0:T(8,128)(2,1)}) %all-gather.10.cloned.1.call-update) | async-done | bytes 4194320 | tf_op jit(solution)/shard_map/all_gather | solution.py:50
  128.1 6.4 copy.46
  134.5 4.1 fusion.25
  138.6 0.1 copy.47
  138.7 0.0 copy-start.10
  138.7 0.0 copy-start.9
  138.7 6.7 convolution_convert_fusion
  145.4 0.0 reduce-scatter.6.cloned.1.call-update
  145.4 0.0 all-gather.8.cloned.1.call-start
  145.5 0.0 copy-done.10
  145.5 43.1 %all-gather.6.cloned.1.call-done = bf16[4096,512]{1,0:T(8,128)(2,1)} async-done(((bf16[128,512]{1,0:T(8,128)(2,1)}), bf16[4096,512]{1,0:T(8,128)(2,1)}) %all-gather.6.cloned.1.call-update) | async-done | bytes 4194320 | tf_op jit(solution)/shard_map/all_gather | solution.py:49
  188.6 6.4 copy.43
  195.0 0.0 copy-done
  195.0 4.1 fusion.28
  199.1 0.0 all-gather.8.cloned.1.call-update
  199.1 0.2 reduce-scatter.10.cloned.1.call-start
  199.4 82.5 %reduce-scatter.6.cloned.1.call-done = bf16[256,128]{1,0:T(8,128)(2,1)} async-done(((bf16[8192,128]{1,0:T(8,128)(2,1)}), bf16[256,128]{1,0:T(8,128)(2,1)}) %reduce-scatter.6.cloned.1.call-update) | async-done | bytes 65552 | tf_op jit(solution)/shard_map/reduce_scatter | solution.py:97
  281.9 0.8 convert_element_type.83
  282.7 0.2 multiply_convert_fusion
  282.9 0.1 copy.48
  283.1 3.2 fusion.6
  286.3 50.8 %all-gather.8.cloned.1.call-done = bf16[8192,128]{1,0:T(8,128)(2,1)} async-done(((bf16[256,128]{1,0:T(8,128)(2,1)}), bf16[8192,128]{1,0:T(8,128)(2,1)}) %all-gather.8.cloned.1.call-update) | async-done | bytes 2097168 | tf_op jit(solution)/shard_map/all_gather | solution.py:58
  337.1 5.7 multiply_reduce_fusion
  342.9 0.1 copy.44
  343.0 0.2 multiply_convert_fusion.1
  343.2 0.1 copy.45
  343.3 3.2 fusion.7
  346.5 7.8 %pad_maximum_fusion = bf16[4096,1024]{0,1:T(8,128)(2,1)} fusion(bf16[4096,512]{0,1:T(8,128)(2,1)} %fusion.7, bf16[4096,512]{0,1:T(8,128)(2,1)} %fusion.6), kind=kLoop, calls=%fused_computation.8 | loop fusion | flops 16777216 | bytes 16777216 | tf_op jit(solution)/shard_map/concatenate | solution.py:112
  354.3 12.0 %copy.51 = bf16[4096,1024]{1,0:T(8,128)(2,1)} copy(bf16[4096,1024]{0,1:T(8,128)(2,1)} %pad_maximum_fusion) | data formatting | bytes 16777216
  366.3 0.0 reduce-scatter.10.cloned.1.call-update
  366.3 0.0 all-reduce.2.cloned.1.call-start
  366.4 1.5 copy-done.5
  367.9 6.1 fusion.2
  374.0 111.0 %reduce-scatter.10.cloned.1.call-done = bf16[128,1024]{1,0:T(8,128)(2,1)} async-done(((bf16[4096,1024]{1,0:T(8,128)(2,1)}), bf16[128,1024]{1,0:T(8,128)(2,1)}) %reduce-scatter.10.cloned.1.call-update) | async-done | bytes 262160
  484.9 1.8 copy.52
  486.7 0.0 all-reduce.2.cloned.1.call-update
  486.7 0.3 reduce-scatter.8.cloned.1.call-start
  487.0 4.8 fusion.3
  491.8 0.0 reduce-scatter.8.cloned.1.call-update
  491.9 5.0 fusion.9
  496.9 0.0 copy-done.4
  496.9 2.6 fusion.8
  499.5 0.0 copy-done.3
  499.5 1.0 copy-done.7
  500.5 1.9 fusion.38
  502.4 60.6 %all-reduce.2.cloned.1.call-done = bf16[128,1024]{0,1:T(8,128)(2,1)} async-done(((bf16[128,1024]{0,1:T(8,128)(2,1)}), bf16[128,1024]{0,1:T(8,128)(2,1)}) %all-reduce.2.cloned.1.call-update) | async-done | bytes 262160 | tf_op jit(solution)/shard_map/psum | solution.py:117
  563.0 1.0 fusion.49
  564.0 0.8 copy.50
  564.8 0.8 copy.49
  565.7 94.6 %reduce-scatter.8.cloned.1.call-done = bf16[256,128]{1,0:T(8,128)(2,1)} async-done(((bf16[8192,128]{1,0:T(8,128)(2,1)}), bf16[256,128]{1,0:T(8,128)(2,1)}) %reduce-scatter.8.cloned.1.call-update) | async-done | bytes 65552 | tf_op jit(solution)/shard_map/reduce_scatter | solution.py:94
  (16 shorter events, 0.0 us)
Async XLA Ops:
  7.2 187.8 %copy-start = (bf16[1,256,4096]{2,1,0:T(8,128)(2,1)S(1)}, bf16[1,256,4096]{2,1,0:T(8,128)(2,1)}, u32[]{:S(2)}) copy-start(bf16[1,256,4096]{2,1,0:T(8,128)(2,1)} %param.11) | copy-start | bytes 6291460
  7.2 61.0 %all-gather.12.cloned.1.call-start = ((), (), s32[]{:S(2)}) async-start(), calls=%async_computation.9 | async-start | bytes 2162688 | tf_op jit(solution)/shard_map/all_gather | solution.py:57
  7.9 120.2 %all-gather.10.cloned.1.call-start = ((), (), s32[]{:S(2)}) async-start(), calls=%async_computation.5 | async-start | bytes 4325376 | tf_op jit(solution)/shard_map/all_gather | solution.py:50
  8.7 179.9 %all-gather.6.cloned.1.call-start = ((), (), s32[]{:S(2)}) async-start(), calls=%async_computation.3 | async-start | bytes 4325376 | tf_op jit(solution)/shard_map/all_gather | solution.py:49
  9.4 272.5 %reduce-scatter.6.cloned.1.call-start = ((), (), s32[]{:S(2)}) async-start(), calls=%async_computation.6 | async-start | bytes 2162688 | tf_op jit(solution)/shard_map/reduce_scatter | solution.py:97
  72.8 3.2 copy-start.2
  138.7 6.8 %copy-start.10 = (s32[1,256,2]{1,2,0:T(2,128)S(1)}, s32[1,256,2]{1,2,0:T(2,128)}, u32[]{:S(2)}) copy-start(s32[1,256,2]{1,2,0:T(2,128)} %param.16) | copy-start | bytes 6148
  138.7 6.8 %copy-start.9 = (f32[1,256,4]{1,2,0:T(4,128)S(1)}, f32[1,256,4]{1,2,0:T(4,128)}, u32[]{:S(2)}) copy-start(f32[1,256,4]{1,2,0:T(4,128)} %param.15) | copy-start | bytes 12292
  145.4 191.7 %all-gather.8.cloned.1.call-start = ((), (), s32[]{:S(2)}) async-start(), calls=%async_computation.4 | async-start | bytes 2162688 | tf_op jit(solution)/shard_map/all_gather | solution.py:58
  199.1 285.8 %reduce-scatter.10.cloned.1.call-start = ((), (), s32[]{:S(2)}) async-start(), calls=%async_computation.10 | async-start | bytes 8650752
  286.3 57.0 %copy-start.6 = (bf16[1,256,4096]{2,1,0:T(8,128)(2,1)S(1)}, bf16[1,256,4096]{2,1,0:T(8,128)(2,1)}, u32[]{:S(2)}) copy-start(bf16[1,256,4096]{2,1,0:T(8,128)(2,1)} %param.21) | copy-start | bytes 6291460
  366.3 1.6 copy-start.5
  366.3 196.7 %all-reduce.2.cloned.1.call-start = ((), (), s32[]{:S(2)}) async-start(), calls=%async_computation.8 | async-start | bytes 524288 | tf_op jit(solution)/shard_map/psum | solution.py:117
  367.9 119.1 %copy-start.8 = (bf16[1,256,128]{2,1,0:T(8,128)(2,1)S(1)}, bf16[1,256,128]{2,1,0:T(8,128)(2,1)}, u32[]{:S(2)}) copy-start(bf16[1,256,128]{2,1,0:T(8,128)(2,1)} %param.12) | copy-start | bytes 196612
  486.7 173.6 %reduce-scatter.8.cloned.1.call-start = ((), (), s32[]{:S(2)}) async-start(), calls=%async_computation.7 | async-start | bytes 2162688 | tf_op jit(solution)/shard_map/reduce_scatter | solution.py:94
  491.9 5.0 copy-start.4
  496.9 2.6 copy-start.3
  496.9 3.6 copy-start.7
  496.9 163.5 %copy-start.1 = (bf16[1,256,4096]{2,1,0:T(8,128)(2,1)S(1)}, bf16[1,256,4096]{2,1,0:T(8,128)(2,1)}, u32[]{:S(2)}) copy-start(bf16[1,256,4096]{2,1,0:T(8,128)(2,1)} %param.11) | copy-start | bytes 6291460
Sparse Core Ops, SparseCore 0:
  10.6 57.5 all-gather.11
  70.7 57.3 all-gather.9
  130.6 57.8 all-gather.5
  192.8 88.9 reduce-scatter.5
  284.8 52.2 all-gather.7
  366.5 118.4 reduce-scatter.9
  488.3 74.6 all-reduce.1
  567.4 92.8 reduce-scatter.7
where the time goes:
time: 668 us; the launch traced here: 667 us
  waiting for transfers between devices  554 us (83%)
  matrix products  52 us (8%)
  local copies, waits for them, and re-layouts  34.1 us (5%)
  between operations  14.3 us (2%)
  other arithmetic  11.8 us (2%)
    unnamed x9, waiting for transfers between devices  113 us
    reduce_scatter x1, waiting for transfers between devices, body(): lax.psum_scatter(key_term.astype(jnp.bfloat16), 'seq', scatter_dimension=...  94.6 us
    reduce_scatter x1, waiting for transfers between devices, body(): lax.psum_scatter(value_term.astype(jnp.bfloat16), 'seq', scatter_dimensio...  82.5 us
    psum x1, waiting for transfers between devices, body(): summed = lax.psum(owned, 'dp').astype(jnp.float32)  60.6 us
    all_gather x1, waiting for transfers between devices, body(): lax.all_gather(own_keys, 'seq', axis=0, tiled=True)  57.3 us
    all_gather x1, waiting for transfers between devices, body(): lax.all_gather(output_panels, 'seq', axis=0, tiled=True)  52.1 us
    all_gather x1, waiting for transfers between devices, body(): lax.all_gather(value_vec, 'seq', axis=0, tiled=True)  50.8 us
    all_gather x1, waiting for transfers between devices, body(): lax.all_gather(value_panels, 'seq', axis=0, tiled=True)  43.1 us
  transfers between devices with their start and end apart: 8, of which 8 were waited for; matrix products, arithmetic and copies ran while one was open for 9% of the time, Pallas kernels for 0%

commit v1 on v0

--- a/solution.py
+++ b/solution.py
@@ -2,6 +2,11 @@
 import jax.numpy as jnp
 from jax import lax
 from jax.sharding import PartitionSpec as P
+
+
+def exchange_gather(shard, axis, along):
+    stack = jnp.stack([shard] * lax.axis_size(axis))
+    return jnp.concatenate(lax.all_to_all(stack, axis, 0, 0), axis=along)
 
 
 def expert_gates(scores, chosen, experts):
@@ -54,7 +59,7 @@
         projection.reshape(tok_rows, experts, head_size) * value_gate[:, :, None], axis=1
     ).astype(jnp.bfloat16)
     keys_all, values_all = (
-        lax.all_gather(own_keys, "seq", axis=0, tiled=True),
+        exchange_gather(own_keys, "seq", 0),
         lax.all_gather(value_vec, "seq", axis=0, tiled=True),
     )
     length = keys_all.shape[0]

time: 668 us -> 637 us (0.954)
  waiting for transfers between devices: 554 us -> 509 us
  starting transfers between devices: 0.72 us -> 12.1 us
    all_to_all x0 -> x1, waiting for transfers between devices: none -> 59.9 us  [exchange_gather(): return jnp.concatenate(lax.all_to_all(stack, axis, 0, 0), axis=along)]
    all_gather x1 -> x0, waiting for transfers between devices: 57.3 us -> none  [body(): lax.all_gather(own_keys, 'seq', axis=0, tiled=True)]
    all_gather x1, waiting for transfers between devices: 52.1 us -> 4.09 us  [body(): lax.all_gather(output_panels, 'seq', axis=0, tiled=True)]
    all_to_all x0 -> x1, starting transfers between devices: none -> 11.4 us  [exchange_gather(): return jnp.concatenate(lax.all_to_all(stack, axis, 0, 0), axis=along)]
    unnamed x26 -> x30, local copies, waits for them, and re-layouts: 19.9 us -> 18.9 us
    unnamed x9 -> x8, waiting for transfers between devices: 113 us -> 112 us
  transfers between devices with their start and end apart: 8 -> 8, of which waited for: 8 -> 8; matrix products, arithmetic and copies ran while one was open for 9% -> 10% of each run, Pallas kernels for 0% -> 0%
where the time goes in v1:
time: 637 us; the launch traced here: 636 us
  waiting for transfers between devices  509 us (80%)
  matrix products  53.5 us (8%)
  local copies, waits for them, and re-layouts  35.8 us (6%)
  between operations  14.4 us (2%)
  starting transfers between devices  12.1 us (2%)
  other arithmetic  10.5 us (2%)
    unnamed x8, waiting for transfers between devices  112 us
    reduce_scatter x1, waiting for transfers between devices, body(): lax.psum_scatter(key_term.astype(jnp.bfloat16), 'seq', scatter_dimension=...  94.6 us
    reduce_scatter x1, waiting for transfers between devices, body(): lax.psum_scatter(value_term.astype(jnp.bfloat16), 'seq', scatter_dimensio...  82.6 us
    all_to_all x1, waiting for transfers between devices, exchange_gather(): return jnp.concatenate(lax.all_to_all(stack, axis, 0, 0), axis=along)  59.9 us
    psum x1, waiting for transfers between devices, body(): summed = lax.psum(owned, 'dp').astype(jnp.float32)  59.6 us
    all_gather x1, waiting for transfers between devices, body(): lax.all_gather(value_vec, 'seq', axis=0, tiled=True)  50.9 us
    all_gather x1, waiting for transfers between devices, body(): lax.all_gather(value_panels, 'seq', axis=0, tiled=True)  45 us
    unnamed x30, local copies, waits for them, and re-layouts  18.9 us
  transfers between devices with their start and end apart: 8, of which 8 were waited for; matrix products, arithmetic and copies ran while one was open for 10% of the time, Pallas kernels for 0%

profile of v1, /device:TPU:8, one launch (start us, length us, event | category | flops | bytes accessed | tf_op | source)
XLA Modules:
  0.0 635.5 jit_solution(11670705400393437149)
XLA Ops:
  7.2 0.0 copy-start
  7.2 0.0 copy-start.10
  7.2 0.0 copy-start.8
  7.2 0.0 copy-start.7
  7.2 0.0 copy-start.12
  7.2 0.0 all-gather.8.cloned.1.call-start
  7.3 0.7 all-gather.8.cloned.1.call-update
  8.0 0.0 all-gather.4.cloned.1.call-start
  8.0 0.7 all-gather.4.cloned.1.call-update
  8.7 2.6 stack.3
  11.3 11.4 %all-to-all-start = ((bf16[32,256,128]{2,1,0:T(8,128)(2,1)}), bf16[32,256,128]{2,1,0:T(8,128)(2,1)}, u32[]{:S(2)}, u32[]{:S(2)}) async-start(bf16[32,256,128]{2,1,0:T(8,128)(2,1)} %stack.3), calls=%async_computation | async-start | bytes 4194304 | tf_op jit(solution)/shard_map/all_to_all | solution.py:9
  22.8 0.0 reduce-scatter.6.cloned.1.call-start
  22.9 0.0 copy-done.10
  22.9 0.0 copy-done.8
  22.9 59.9 %all-to-all-done = bf16[32,256,128]{2,1,0:T(8,128)(2,1)} async-done(((bf16[32,256,128]{2,1,0:T(8,128)(2,1)}), bf16[32,256,128]{2,1,0:T(8,128)(2,1)}, u32[]{:S(2)}, u32[]{:S(2)}) %all-to-all-start) | async-done | bytes 2097184 | tf_op jit(solution)/shard_map/all_to_all | solution.py:9
  82.8 0.0 copy-done.7
  82.8 4.7 fusion.40
  87.5 1.4 exponential_reduce_fusion
  88.9 1.9 copy-done.2
  90.7 4.1 all-gather.8.cloned.1.call-done
  94.8 6.4 %copy.46 = bf16[512,4096]{1,0:T(8,128)(2,1)} copy(bf16[512,4096]{0,1:T(8,128)(2,1)} %bitcast.70) | data formatting | bytes 8388608 | tf_op jit(solution)/shard_map/dot_general | solution.py:86
  101.2 4.1 fusion.22
  105.3 0.1 copy.47
  105.5 0.0 copy-start.11
  105.5 0.0 copy-start.9
  105.5 6.5 %convolution_convert_fusion = bf16[8192,128]{1,0:T(8,128)(2,1)} fusion(bf16[256,128]{0,1:T(8,128)(2,1)S(1)} %copy.47, f32[256,8192]{1,0:T(8,128)} %copy-done.2, f32[256]{0:T(256)S(1)} %log_add_fusion), kind=kOutput, calls=%fused_computation.7 | convolution fusion | flops 542113792 | bytes 10552320 | tf_op jit(solution)/shard_map/dot_general | solution.py:24
  112.0 0.0 reduce-scatter.6.cloned.1.call-update
  112.0 0.0 all-gather.6.cloned.1.call-start
  112.1 45.0 %all-gather.4.cloned.1.call-done = bf16[4096,512]{1,0:T(8,128)(2,1)} async-done(((bf16[128,512]{1,0:T(8,128)(2,1)}), bf16[4096,512]{1,0:T(8,128)(2,1)}) %all-gather.4.cloned.1.call-update) | async-done | bytes 4194320 | tf_op jit(solution)/shard_map/all_gather | solution.py:54
  157.2 6.4 %copy.43 = bf16[512,4096]{1,0:T(8,128)(2,1)} copy(bf16[512,4096]{0,1:T(8,128)(2,1)} %bitcast.71) | data formatting | bytes 8388608 | tf_op jit(solution)/shard_map/dot_general | solution.py:57
  163.6 4.1 fusion.25
  167.7 0.0 all-gather.6.cloned.1.call-update
  167.7 0.2 reduce-scatter.10.cloned.1.call-start
  167.9 82.6 %reduce-scatter.6.cloned.1.call-done = bf16[256,128]{1,0:T(8,128)(2,1)} async-done(((bf16[8192,128]{1,0:T(8,128)(2,1)}), bf16[256,128]{1,0:T(8,128)(2,1)}) %reduce-scatter.6.cloned.1.call-update) | async-done | bytes 65552 | tf_op jit(solution)/shard_map/reduce_scatter | solution.py:102
  250.5 0.8 convert_element_type.83
  251.4 0.2 multiply_convert_fusion
  251.6 0.1 copy.48
  251.7 3.2 fusion.6
  254.9 50.9 %all-gather.6.cloned.1.call-done = bf16[8192,128]{1,0:T(8,128)(2,1)} async-done(((bf16[256,128]{1,0:T(8,128)(2,1)}), bf16[8192,128]{1,0:T(8,128)(2,1)}) %all-gather.6.cloned.1.call-update) | async-done | bytes 2097168 | tf_op jit(solution)/shard_map/all_gather | solution.py:63
  305.8 5.7 multiply_reduce_fusion
  311.5 0.1 copy.44
  311.6 0.2 multiply_convert_fusion.1
  311.9 0.1 copy.45
  312.0 3.2 fusion.7
  315.2 7.8 %pad_maximum_fusion = bf16[4096,1024]{0,1:T(8,128)(2,1)} fusion(bf16[4096,512]{0,1:T(8,128)(2,1)} %fusion.7, bf16[4096,512]{0,1:T(8,128)(2,1)} %fusion.6), kind=kLoop, calls=%fused_computation.8 | loop fusion | flops 16777216 | bytes 16777216 | tf_op jit(solution)/shard_map/concatenate | solution.py:117
  323.0 12.0 %copy.51 = bf16[4096,1024]{1,0:T(8,128)(2,1)} copy(bf16[4096,1024]{0,1:T(8,128)(2,1)} %pad_maximum_fusion) | data formatting | bytes 16777216
  335.0 0.0 reduce-scatter.10.cloned.1.call-update
  335.0 0.0 all-reduce.2.cloned.1.call-start
  335.1 1.5 copy-done.5
  336.6 6.0 fusion.2
  342.6 111.0 %reduce-scatter.10.cloned.1.call-done = bf16[128,1024]{1,0:T(8,128)(2,1)} async-done(((bf16[4096,1024]{1,0:T(8,128)(2,1)}), bf16[128,1024]{1,0:T(8,128)(2,1)}) %reduce-scatter.10.cloned.1.call-update) | async-done | bytes 262160
  453.7 1.8 copy.52
  455.4 0.0 all-reduce.2.cloned.1.call-update
  455.5 0.3 reduce-scatter.8.cloned.1.call-start
  455.7 4.8 fusion.3
  460.6 0.0 reduce-scatter.8.cloned.1.call-update
  460.6 5.0 fusion.9
  465.6 2.6 fusion.8
  468.2 3.5 fusion.30
  471.7 59.6 %all-reduce.2.cloned.1.call-done = bf16[128,1024]{0,1:T(8,128)(2,1)} async-done(((bf16[128,1024]{0,1:T(8,128)(2,1)}), bf16[128,1024]{0,1:T(8,128)(2,1)}) %all-reduce.2.cloned.1.call-update) | async-done | bytes 262160 | tf_op jit(solution)/shard_map/psum | solution.py:122
  531.4 1.0 fusion.39
  532.4 0.8 copy.50
  533.2 0.8 copy.49
  534.0 94.6 %reduce-scatter.8.cloned.1.call-done = bf16[256,128]{1,0:T(8,128)(2,1)} async-done(((bf16[8192,128]{1,0:T(8,128)(2,1)}), bf16[256,128]{1,0:T(8,128)(2,1)}) %reduce-scatter.8.cloned.1.call-update) | async-done | bytes 65552 | tf_op jit(solution)/shard_map/reduce_scatter | solution.py:99
  (20 shorter events, 0.1 us)
Async XLA Ops:
  7.2 156.4 %copy-start = (bf16[1,256,4096]{2,1,0:T(8,128)(2,1)S(1)}, bf16[1,256,4096]{2,1,0:T(8,128)(2,1)}, u32[]{:S(2)}) copy-start(bf16[1,256,4096]{2,1,0:T(8,128)(2,1)} %param.11) | copy-start | bytes 6291460
  7.2 15.7 %copy-start.10 = (s32[1,256,2]{1,2,0:T(2,128)S(1)}, s32[1,256,2]{1,2,0:T(2,128)}, u32[]{:S(2)}) copy-start(s32[1,256,2]{1,2,0:T(2,128)} %param.18) | copy-start | bytes 6148
  7.2 15.7 %copy-start.8 = (f32[1,256,4]{1,2,0:T(4,128)S(1)}, f32[1,256,4]{1,2,0:T(4,128)}, u32[]{:S(2)}) copy-start(f32[1,256,4]{1,2,0:T(4,128)} %param.17) | copy-start | bytes 12292
  7.2 75.6 %copy-start.7 = (bf16[1,256,128]{2,1,0:T(8,128)(2,1)S(1)}, bf16[1,256,128]{2,1,0:T(8,128)(2,1)}, u32[]{:S(2)}) copy-start(bf16[1,256,128]{2,1,0:T(8,128)(2,1)} %param.12) | copy-start | bytes 196612
  7.2 75.6 %copy-start.12 = (s32[1,256]{1,0:T(1,128)S(1)}, s32[1,256]{1,0:T(1,128)}, u32[]{:S(2)}) copy-start(s32[1,256]{1,0:T(1,128)} %param.14) | copy-start | bytes 3076
  7.2 87.6 %all-gather.8.cloned.1.call-start = ((), (), s32[]{:S(2)}) async-start(), calls=%async_computation.6 | async-start | bytes 4325376 | tf_op jit(solution)/shard_map/all_gather | solution.py:55
  8.0 149.2 %all-gather.4.cloned.1.call-start = ((), (), s32[]{:S(2)}) async-start(), calls=%async_computation.4 | async-start | bytes 4325376 | tf_op jit(solution)/shard_map/all_gather | solution.py:54
  11.3 71.5 %all-to-all-start = ((bf16[32,256,128]{2,1,0:T(8,128)(2,1)}), bf16[32,256,128]{2,1,0:T(8,128)(2,1)}, u32[]{:S(2)}, u32[]{:S(2)}) async-start(bf16[32,256,128]{2,1,0:T(8,128)(2,1)} %stack.3), calls=%async_computation | async-start | bytes 4194304 | tf_op jit(solution)/shard_map/all_to_all | solution.py:9
  22.8 227.7 %reduce-scatter.6.cloned.1.call-start = ((), (), s32[]{:S(2)}) async-start(), calls=%async_computation.7 | async-start | bytes 2162688 | tf_op jit(solution)/shard_map/reduce_scatter | solution.py:102
  87.5 3.2 copy-start.2
  105.5 6.6 %copy-start.11 = (s32[1,256,2]{1,2,0:T(2,128)S(1)}, s32[1,256,2]{1,2,0:T(2,128)}, u32[]{:S(2)}) copy-start(s32[1,256,2]{1,2,0:T(2,128)} %param.16) | copy-start | bytes 6148
  105.5 6.6 %copy-start.9 = (f32[1,256,4]{1,2,0:T(4,128)S(1)}, f32[1,256,4]{1,2,0:T(4,128)}, u32[]{:S(2)}) copy-start(f32[1,256,4]{1,2,0:T(4,128)} %param.15) | copy-start | bytes 12292
  112.0 193.8 %all-gather.6.cloned.1.call-start = ((), (), s32[]{:S(2)}) async-start(), calls=%async_computation.5 | async-start | bytes 2162688 | tf_op jit(solution)/shard_map/all_gather | solution.py:63
  167.7 285.9 %reduce-scatter.10.cloned.1.call-start = ((), (), s32[]{:S(2)}) async-start(), calls=%async_computation.10 | async-start | bytes 8650752
  254.9 57.1 %copy-start.6 = (bf16[1,256,4096]{2,1,0:T(8,128)(2,1)S(1)}, bf16[1,256,4096]{2,1,0:T(8,128)(2,1)}, u32[]{:S(2)}) copy-start(bf16[1,256,4096]{2,1,0:T(8,128)(2,1)} %param.21) | copy-start | bytes 6291460
  335.0 1.6 copy-start.5
  335.0 196.3 %all-reduce.2.cloned.1.call-start = ((), (), s32[]{:S(2)}) async-start(), calls=%async_computation.9 | async-start | bytes 524288 | tf_op jit(solution)/shard_map/psum | solution.py:122
  455.5 173.2 %reduce-scatter.8.cloned.1.call-start = ((), (), s32[]{:S(2)}) async-start(), calls=%async_computation.8 | async-start | bytes 2162688 | tf_op jit(solution)/shard_map/reduce_scatter | solution.py:99
  460.6 5.0 copy-start.4
  465.6 2.6 copy-start.3
  465.6 163.1 %copy-start.1 = (bf16[1,256,4096]{2,1,0:T(8,128)(2,1)S(1)}, bf16[1,256,4096]{2,1,0:T(8,128)(2,1)}, u32[]{:S(2)}) copy-start(bf16[1,256,4096]{2,1,0:T(8,128)(2,1)} %param.11) | copy-start | bytes 6291460
Sparse Core Ops, SparseCore 0:
  10.6 84.1 all-gather.7
  97.4 59.7 all-gather.3
  161.6 88.8 reduce-scatter.5
  253.5 52.2 all-gather.5
  335.2 118.4 reduce-scatter.9
  456.9 74.4 all-reduce.1
  535.8 92.8 reduce-scatter.7
